TPU v7x, 32 devices: a whole 2x2x4 slice. The times are simulated.
32 devices in a mesh: ka: 8 (over z, x), band: 4 (over y, core).
Axes of the slice: x: 2, y: 2, z: 4, core: 2. Of those that a mesh axis runs over, the one named last changes fastest.
Arguments:
- occupied: bfloat16 [16, 8, 4096], P('ka'), may hold values from -6 to 6
- virtual: bfloat16 [16, 128, 4096], P('ka', 'band'), may hold values from -6 to 6
- occ_energy: float32 [16, 8], P('ka'), may hold values from -2 to -0.5
- virt_energy: float32 [16, 128], P(None, 'band'), may hold values from 0.5 to 2
- partner: int32 [2, 16], replicated, may hold values from 0 to 15, as said below
- coulomb: float32 [2, 512], replicated, may hold values from 0.5 to 2
- basis: bfloat16 [512, 4096], replicated, may hold values from -0.09375 to 0.09375
Outputs:
- occ_update: bfloat16 [16, 8, 4096], P('ka', None, 'band')
- virt_update: bfloat16 [16, 128, 4096], P('ka', 'band')
Inputs may be any that keep to these rules, and one draw needn't show every extreme that they name: Each row pairs the 16 k-points: partner[q, partner[q, k]] == k and partner[q, k] != k.
All inputs are finite; a program needn't handle non-finite values.
Results may differ from a plain program's by a relative error of at most 0.012.
Values may be sent and summed in bfloat16 or wider, within the bound.
No kernel may reach another device: no remote copies, remote signals or barrier semaphores. Data moves between devices by JAX's collectives and lax.ppermute only.
A program may use at most 64 MiB of HBM per device.

v0:
```python
import math
import jax
import jax.numpy as jnp
from jax import lax
from jax.sharding import PartitionSpec as P

FREQUENCY = 2.5
BROADENING = 0.4


def response(energy_gaps):
    shifted = FREQUENCY - energy_gaps
    return shifted / (shifted * shifted + BROADENING * BROADENING)


def contract_grid(left, right):
    return lax.dot_general(
        left, right, (((1,), (1,)), ((), ())), preferred_element_type=jnp.float32
    )


def contract_rows(left, right):
    return lax.dot_general(
        left, right, (((0,), (0,)), ((), ())), preferred_element_type=jnp.float32
    )


def shards(occupied, virtual, occ_energy, virt_energy, partner, coulomb, basis):
    local_k, occ_count, grid_count = occupied.shape
    group_count = virtual.shape[1]
    aux_count = basis.shape[0]
    transfers = partner.shape[0]
    ka_size = lax.axis_size("ka")
    band_size = lax.axis_size("band")
    total_k = local_k * ka_size
    virt_count = group_count * band_size
    slice_width = group_count * grid_count // ka_size
    gram_scale = 1.0 / math.sqrt(total_k * occ_count * virt_count * aux_count)
    occ_scale = 1.0 / math.sqrt(transfers * virt_count)
    own_k = lax.axis_index("ka") * local_k + jnp.arange(local_k, dtype=jnp.int32)

    def regroup(slices):
        picked = jnp.stack(
            [jnp.take(slices, partner[transfer], axis=0) for transfer in range(transfers)]
        )
        return lax.all_to_all(picked, "ka", split_axis=1, concat_axis=2, tiled=True)

    routed = regroup(
        lax.all_to_all(
            virtual.reshape(local_k, ka_size, slice_width),
            "ka",
            split_axis=1,
            concat_axis=0,
            tiled=True,
        )
    )
    partner_virt = routed.reshape(transfers, local_k, group_count, grid_count)
    partner_energy = jnp.take(virt_energy, jnp.take(partner, own_k, axis=1), axis=0)
    occ_total = jnp.zeros((local_k, occ_count, grid_count), jnp.float32)
    virt_terms = []
    for transfer in range(transfers):
        pair_rows = (occupied[:, :, None, :] * partner_virt[transfer][:, None, :, :]).reshape(
            -1, grid_count
        )
        project_coeffs = contract_grid(pair_rows, basis).astype(jnp.bfloat16)
        energy_gaps = partner_energy[transfer][:, None, :] - occ_energy[:, :, None]
        weights = response(energy_gaps).reshape(-1, 1)
        weighted = (project_coeffs.astype(jnp.float32) * weights).astype(jnp.bfloat16)
        gram_block = contract_rows(weighted, project_coeffs)
        coul_rows = coulomb[transfer : transfer + 1]
        totals = lax.psum(gram_block[None], ("ka", "band"))
        screen_block = (coul_rows[:, :, None] * totals * coul_rows[:, None, :] * gram_scale).astype(
            jnp.bfloat16
        )[0]
        screened = jnp.dot(project_coeffs, screen_block, preferred_element_type=jnp.float32).astype(
            jnp.bfloat16
        )
        grid_field = jnp.dot(screened, basis, preferred_element_type=jnp.float32).astype(
            jnp.bfloat16
        )
        grid_field = grid_field.reshape(local_k, occ_count, group_count, grid_count).astype(
            jnp.float32
        )
        occ_term = jnp.sum(
            grid_field * partner_virt[transfer][:, None, :, :].astype(jnp.float32), axis=2
        )
        virt_term = jnp.sum(
            grid_field * occupied[:, :, None, :].astype(jnp.float32), axis=1
        ).astype(jnp.bfloat16)
        occ_term, virt_term = (occ_term, virt_term)
        occ_total = occ_total + occ_term
        virt_terms.append(virt_term)
    stacked = jnp.stack(virt_terms).reshape(transfers, local_k, ka_size, slice_width)
    slices = lax.all_to_all(stacked, "ka", split_axis=2, concat_axis=1, tiled=True)
    returned = jnp.take(slices[0], partner[0], axis=0).astype(jnp.float32)
    transfer = 1
    returned = returned + jnp.take(slices[transfer], partner[transfer], axis=0).astype(jnp.float32)
    home_rows = lax.all_to_all(
        returned.astype(jnp.bfloat16), "ka", split_axis=0, concat_axis=1, tiled=True
    )
    virt_update = home_rows.reshape(local_k, group_count, grid_count)
    occ_share = lax.psum_scatter(
        occ_total.astype(jnp.bfloat16), "band", scatter_dimension=2, tiled=True
    ).astype(jnp.float32)
    return ((occ_share * occ_scale).astype(jnp.bfloat16), virt_update)


def solution(mesh):
    in_specs = (
        P("ka", None, None),
        P("ka", "band", None),
        P("ka", None),
        P(None, "band"),
        P(),
        P(),
        P(),
    )
    out_specs = (P("ka", None, "band"), P("ka", "band", None))
    return jax.shard_map(shards, mesh=mesh, in_specs=in_specs, out_specs=out_specs, check_vma=False)
```

profile of v0, /device:TPU:0, one launch (start us, length us, event | category | flops | bytes accessed | tf_op | source)
XLA Modules:
  0.0 310.9 jit_solution(7381379015960021521)
XLA Ops:
  7.2 1.5 reshape.231
  8.6 1.3 copy.50
  10.0 7.3 %all-to-all-start = ((bf16[2,8,16384]{2,0,1:T(2,128)(2,1)}), bf16[2,8,16384]{2,0,1:T(2,128)(2,1)S(1)}, u32[]{:S(2)}, u32[]{:S(2)}) async-start(bf16[2,8,16384]{2,0,1:T(2,128)(2,1)} %copy.50), calls=%async_computation | async-start | bytes 1048576 | tf_op jit(solution)/shard_map/all_to_all | solution.py:49
  18.1 13.7 %all-to-all-done = bf16[2,8,16384]{2,0,1:T(2,128)(2,1)S(1)} async-done(((bf16[2,8,16384]{2,0,1:T(2,128)(2,1)}), bf16[2,8,16384]{2,0,1:T(2,128)(2,1)S(1)}, u32[]{:S(2)}, u32[]{:S(2)}) %all-to-all-start) | async-done | bytes 524320 | tf_op jit(solution)/shard_map/all_to_all | solution.py:49
  34.0 2.0 copy.51
  36.1 3.6 %all-to-all-start.1 = ((bf16[2,16,1,16384]{3,0,2,1:T(2,128)(2,1)}), bf16[2,16,1,16384]{3,0,2,1:T(2,128)(2,1)S(1)}, u32[]{:S(2)}, u32[]{:S(2)}) async-start(bf16[2,16,1,16384]{3,0,2,1:T(2,128)(2,1)} %copy.51), calls=%async_computation.1 | async-start | bytes 2097152 | tf_op jit(solution)/shard_map/all_to_all | solution.py:46
  41.7 24.0 %all-to-all-done.1 = bf16[2,16,1,16384]{3,0,2,1:T(2,128)(2,1)S(1)} async-done(((bf16[2,16,1,16384]{3,0,2,1:T(2,128)(2,1)}), bf16[2,16,1,16384]{3,0,2,1:T(2,128)(2,1)S(1)}, u32[]{:S(2)}, u32[]{:S(2)}) %all-to-all-start.1) | async-done | bytes 1048608 | tf_op jit(solution)/shard_map/all_to_all | solution.py:46
  65.7 1.7 fusion.32
  70.1 1.4 copy-done.1
  71.6 2.4 convolution_convert_fusion.3
  73.9 2.4 convolution_convert_fusion.5
  76.3 1.6 convolution_bitcast_fusion
  77.9 1.6 convolution_bitcast_fusion.1
  80.7 132.6 %all-reduce.3.cloned.1.call-done = (f32[1,512,512]{2,1,0:T(8,128)}, f32[1,512,512]{2,1,0:T(8,128)}) async-done(((f32[1,512,512]{2,1,0:T(8,128)}, f32[1,512,512]{2,1,0:T(8,128)}), (f32[1,512,512]{2,1,0:T(8,128)}, f32[1,512,512]{2,1,0:T(8,128)})) %all-reduce.3.cloned.1.call-update) | async-done | bytes 2097168 | tf_op jit(solution)/shard_map/psum | solution.py:71
  213.3 7.6 %fusion.2 = (f32[2,8,4096]{2,1,0:T(8,128)S(1)}, bf16[512,4096]{1,0:T(8,128)(2,1)}) fusion(f32[2,32,4096]{2,1,0:T(8,128)} %convert_element_type.132, bf16[512,4096]{1,0:T(8,128)(2,1)} %param.15, bf16[512,512]{1,0:T(8,128)(2,1)S(1)} %convolution_convert_fusion.3, f32[1,512,512]{2,1,0:T(8,128)} %get-tuple-element.6, f32[512]{0:T(512)S(1)} %bitcast.114), kind=kOutput, calls=%fused_computation.12 | convolution fusion | flops 2425552896 | bytes 11274240 | tf_op jit(solution)/shard_map/dot_general | solution.py:78
  220.9 7.6 %fusion = (f32[2,8,4096]{2,1,0:T(8,128)S(1)}, bf16[512,4096]{1,0:T(8,128)(2,1)}) fusion(f32[2,32,4096]{2,1,0:T(8,128)S(1)} %convert_element_type.123, bf16[512,4096]{1,0:T(8,128)(2,1)} %param.15, bf16[512,512]{1,0:T(8,128)(2,1)S(1)} %convolution_convert_fusion.5, f32[1,512,512]{2,1,0:T(8,128)} %get-tuple-element.5, f32[512]{0:T(512)S(1)} %bitcast.113), kind=kOutput, calls=%fused_computation.10 | convolution fusion | flops 2425552896 | bytes 11274240 | tf_op jit(solution)/shard_map/dot_general | solution.py:78
  228.5 4.6 %fusion.1 = (bf16[2,32,4096]{2,1,0:T(8,128)(2,1)S(1)}, bf16[2,32,4096]{2,1,0:T(8,128)(2,1)S(1)}) fusion(bf16[2,8,32,4096]{3,2,1,0:T(8,128)(2,1)} %bitcast.106, f32[2,8,4096]{2,1,0:T(8,128)S(1)} %convert_element_type.136, bf16[2,8,32,4096]{3,2,1,0:T(8,128)(2,1)} %bitcast.105), kind=kLoop, calls=%fused_computation.11 | loop fusion | flops 12058624 | bytes 9699328 | tf_op jit(solution)/shard_map/reduce_sum | solution.py:87
  235.2 28.1 %all_to_all.63 = bf16[2,2,8,16384]{3,1,0,2:T(2,128)(2,1)S(1)} all-to-all(bf16[2,2,8,16384]{3,1,0,2:T(2,128)(2,1)S(1)} %copy.57), channel_id=1, replica_groups=mesh['ka'=8,'band'=4] {'ka'}, dimensions={2} | all-to-all | bytes 2097152 | tf_op jit(solution)/shard_map/all_to_all | solution.py:94
  268.0 1.1 reshape.317
  269.1 3.6 %all-to-all-start.3 = ((bf16[8,2,16384]{2,1,0:T(2,128)(2,1)}), bf16[8,2,16384]{2,1,0:T(2,128)(2,1)S(1)}, u32[]{:S(2)}, u32[]{:S(2)}) async-start(bf16[8,2,16384]{2,1,0:T(2,128)(2,1)} %reshape.317), calls=%async_computation.4 | async-start | bytes 1048576 | tf_op jit(solution)/shard_map/all_to_all | solution.py:98
  273.5 23.5 %reduce-scatter.2.cloned.1.call-done = bf16[2,8,1024]{2,1,0:T(8,128)(2,1)} async-done(((bf16[2,8,4096]{2,1,0:T(8,128)(2,1)}), bf16[2,8,1024]{2,1,0:T(8,128)(2,1)}) %reduce-scatter.2.cloned.1.call-update) | async-done | bytes 32784 | tf_op jit(solution)/shard_map/reduce_scatter | solution.py:102
  297.0 1.4 multiply_convert_fusion.6
  298.9 3.3 %reduce = bf16[16,16384]{1,0:T(8,128)(2,1)S(1)} reduce(bf16[16,1,16384]{2,1,0:T(2,128)(2,1)S(1)} %reshape.318, bf16[]{:T(256)} %constant.60), dimensions={1}, to_apply=%all_to_all.56.reduce_sub_computation | reduce | bytes 1048578 | tf_op jit(solution)/shard_map/all_to_all | solution.py:98
  302.8 1.2 reshape.232
  (68 shorter events, 17.5 us)
Async XLA Ops:
  7.2 33.6 %copy-start = (f32[16,32]{1,0:T(8,128)S(1)}, f32[16,32]{1,0:T(8,128)}, u32[]{:S(2)}) copy-start(f32[16,32]{1,0:T(8,128)} %param.12) | copy-start | bytes 6148
  10.0 21.8 %all-to-all-start = ((bf16[2,8,16384]{2,0,1:T(2,128)(2,1)}), bf16[2,8,16384]{2,0,1:T(2,128)(2,1)S(1)}, u32[]{:S(2)}, u32[]{:S(2)}) async-start(bf16[2,8,16384]{2,0,1:T(2,128)(2,1)} %copy.50), calls=%async_computation | async-start | bytes 1048576 | tf_op jit(solution)/shard_map/all_to_all | solution.py:49
  33.7 6.0 %copy-start.3 = (s32[2,16]{1,0:T(2,128)S(1)}, s32[2,16]{1,0:T(2,128)}, u32[]{:S(2)}) copy-start(s32[2,16]{1,0:T(2,128)} %param.13) | copy-start | bytes 388
  33.7 7.7 %copy-start.5 = (f32[2,8]{1,0:T(2,128)S(1)}, f32[2,8]{1,0:T(2,128)}, u32[]{:S(2)}) copy-start(f32[2,8]{1,0:T(2,128)} %param.11) | copy-start | bytes 196
  36.1 29.6 %all-to-all-start.1 = ((bf16[2,16,1,16384]{3,0,2,1:T(2,128)(2,1)}), bf16[2,16,1,16384]{3,0,2,1:T(2,128)(2,1)S(1)}, u32[]{:S(2)}, u32[]{:S(2)}) async-start(bf16[2,16,1,16384]{3,0,2,1:T(2,128)(2,1)} %copy.51), calls=%async_computation.1 | async-start | bytes 2097152 | tf_op jit(solution)/shard_map/all_to_all | solution.py:46
  39.7 173.6 %all-reduce.3.cloned.1.call-start = ((), (), s32[]{:S(2)}) async-start(), calls=%async_computation.6 | async-start | bytes 4194304 | tf_op jit(solution)/shard_map/psum | solution.py:71
  65.7 3.7 %copy-start.2 = (bf16[2,8,4096]{2,1,0:T(8,128)(2,1)S(1)}, bf16[2,8,4096]{2,1,0:T(8,128)(2,1)}, u32[]{:S(2)}) copy-start(bf16[2,8,4096]{2,1,0:T(8,128)(2,1)} %param.9) | copy-start | bytes 393220
  69.4 2.2 copy-start.1
  76.3 3.2 %copy-start.4 = (f32[2,512]{1,0:T(2,128)S(1)}, f32[2,512]{1,0:T(2,128)}, u32[]{:S(2)}) copy-start(f32[2,512]{1,0:T(2,128)} %param.14) | copy-start | bytes 12292
  269.1 29.2 %all-to-all-start.3 = ((bf16[8,2,16384]{2,1,0:T(2,128)(2,1)}), bf16[8,2,16384]{2,1,0:T(2,128)(2,1)S(1)}, u32[]{:S(2)}, u32[]{:S(2)}) async-start(bf16[8,2,16384]{2,1,0:T(2,128)(2,1)} %reshape.317), calls=%async_computation.4 | async-start | bytes 1048576 | tf_op jit(solution)/shard_map/all_to_all | solution.py:98
  272.7 24.2 %reduce-scatter.2.cloned.1.call-start = ((), (), s32[]{:S(2)}) async-start(), calls=%async_computation.5 | async-start | bytes 163840 | tf_op jit(solution)/shard_map/reduce_scatter | solution.py:102
Sparse Core Ops, SparseCore 0:
  79.6 133.6 all-reduce.2
  276.0 20.9 reduce-scatter.1
where the time goes:
time: 311 us
  waiting for transfers between devices  194 us (62%)
  blocking collectives  28.1 us (9%)
  matrix products  23 us (7%)
  local copies, waits for them, and re-layouts  22.5 us (7%)
  starting transfers between devices  14.6 us (5%)
  other arithmetic  14.6 us (5%)
  between operations  14.3 us (5%)
    psum x1, waiting for transfers between devices, shards(): totals = lax.psum(gram_block[None], ('ka', 'band'))  133 us
    all_to_all x1, blocking collectives, shards(): lax.all_to_all(stacked, 'ka', split_axis=2, concat_axis=1, tiled=True)  28.1 us
    all_to_all x1, waiting for transfers between devices, regroup(): return lax.all_to_all(picked, 'ka', split_axis=1, concat_axis=2, tiled=True)  24 us
    reduce_scatter x1, waiting for transfers between devices, shards(): lax.psum_scatter(occ_total.astype(jnp.bfloat16), 'band', scatter_dimensio...  23.5 us
    dot_general x2, matrix products, shards(): jnp.dot(screened, basis, preferred_element_type=jnp.float32)  15.2 us
    all_to_all x1, waiting for transfers between devices, shards(): lax.all_to_all(virtual.reshape(local_k, ka_size, slice_width), 'ka', spli...  13.7 us
    all_to_all x1, starting transfers between devices, shards(): lax.all_to_all(virtual.reshape(local_k, ka_size, slice_width), 'ka', spli...  7.28 us
  transfers between devices with their start and end apart: 5, of which 4 were waited for; matrix products, arithmetic and copies ran while one was open for 2% of the time, Pallas kernels for 0%

commit v1 on v0

--- a/solution.py
+++ b/solution.py
@@ -68,7 +68,7 @@
         weighted = (project_coeffs.astype(jnp.float32) * weights).astype(jnp.bfloat16)
         gram_block = contract_rows(weighted, project_coeffs)
         coul_rows = coulomb[transfer : transfer + 1]
-        totals = lax.psum(gram_block[None], ("ka", "band"))
+        totals = lax.psum(lax.psum(gram_block[None], "band"), "ka")
         screen_block = (coul_rows[:, :, None] * totals * coul_rows[:, None, :] * gram_scale).astype(
             jnp.bfloat16
         )[0]

time: 311 us -> 335 us (1.077)
  waiting for transfers between devices: 194 us -> 216 us
    psum x1 -> x2, waiting for transfers between devices: 133 us -> 155 us  [shards(): totals = lax.psum(lax.psum(gram_block[None], 'band'), 'ka')]
  transfers between devices with their start and end apart: 5 -> 6, of which waited for: 4 -> 5; matrix products, arithmetic and copies ran while one was open for 2% -> 2% of each run, Pallas kernels for 0% -> 0%
where the time goes in v1:
time: 335 us; the launch traced here: 334 us
  waiting for transfers between devices  216 us (64%)
  blocking collectives  29.4 us (9%)
  matrix products  22.8 us (7%)
  local copies, waits for them, and re-layouts  22.3 us (7%)
  starting transfers between devices  15.3 us (5%)
  other arithmetic  14.6 us (4%)
  between operations  14.1 us (4%)
    psum x2, waiting for transfers between devices, shards(): totals = lax.psum(lax.psum(gram_block[None], 'band'), 'ka')  155 us
    all_to_all x1, blocking collectives, shards(): lax.all_to_all(stacked, 'ka', split_axis=2, concat_axis=1, tiled=True)  29.4 us
    all_to_all x1, waiting for transfers between devices, regroup(): return lax.all_to_all(picked, 'ka', split_axis=1, concat_axis=2, tiled=True)  23.8 us
    reduce_scatter x1, waiting for transfers between devices, shards(): lax.psum_scatter(occ_total.astype(jnp.bfloat16), 'band', scatter_dimensio...  23.3 us
    dot_general x2, matrix products, shards(): jnp.dot(screened, basis, preferred_element_type=jnp.float32)  15 us
    all_to_all x1, waiting for transfers between devices, shards(): lax.all_to_all(virtual.reshape(local_k, ka_size, slice_width), 'ka', spli...  13.7 us
    all_to_all x1, starting transfers between devices, shards(): lax.all_to_all(virtual.reshape(local_k, ka_size, slice_width), 'ka', spli...  7.28 us
  transfers between devices with their start and end apart: 6, of which 5 were waited for; matrix products, arithmetic and copies ran while one was open for 2% of the time, Pallas kernels for 0%

profile of v1, /device:TPU:0, one launch (start us, length us, event | category | flops | bytes accessed | tf_op | source)
XLA Modules:
  0.0 334.5 jit_solution(12075152669586633961)
XLA Ops:
  7.2 1.5 reshape.231
  8.6 1.3 copy.50
  10.0 7.3 %all-to-all-start = ((bf16[2,8,16384]{2,0,1:T(2,128)(2,1)}), bf16[2,8,16384]{2,0,1:T(2,128)(2,1)S(1)}, u32[]{:S(2)}, u32[]{:S(2)}) async-start(bf16[2,8,16384]{2,0,1:T(2,128)(2,1)} %copy.50), calls=%async_computation | async-start | bytes 1048576 | tf_op jit(solution)/shard_map/all_to_all | solution.py:49
  18.1 13.7 %all-to-all-done = bf16[2,8,16384]{2,0,1:T(2,128)(2,1)S(1)} async-done(((bf16[2,8,16384]{2,0,1:T(2,128)(2,1)}), bf16[2,8,16384]{2,0,1:T(2,128)(2,1)S(1)}, u32[]{:S(2)}, u32[]{:S(2)}) %all-to-all-start) | async-done | bytes 524320 | tf_op jit(solution)/shard_map/all_to_all | solution.py:49
  34.0 2.0 copy.51
  36.1 3.6 %all-to-all-start.1 = ((bf16[2,16,1,16384]{3,0,2,1:T(2,128)(2,1)}), bf16[2,16,1,16384]{3,0,2,1:T(2,128)(2,1)S(1)}, u32[]{:S(2)}, u32[]{:S(2)}) async-start(bf16[2,16,1,16384]{3,0,2,1:T(2,128)(2,1)} %copy.51), calls=%async_computation.1 | async-start | bytes 2097152 | tf_op jit(solution)/shard_map/all_to_all | solution.py:46
  41.9 23.8 %all-to-all-done.1 = bf16[2,16,1,16384]{3,0,2,1:T(2,128)(2,1)S(1)} async-done(((bf16[2,16,1,16384]{3,0,2,1:T(2,128)(2,1)}), bf16[2,16,1,16384]{3,0,2,1:T(2,128)(2,1)S(1)}, u32[]{:S(2)}, u32[]{:S(2)}) %all-to-all-start.1) | async-done | bytes 1048608 | tf_op jit(solution)/shard_map/all_to_all | solution.py:46
  65.6 1.5 fusion.32
  70.0 1.4 copy-done.1
  71.4 2.4 convolution_convert_fusion.3
  73.8 2.4 convolution_convert_fusion.5
  76.1 1.6 convolution_bitcast_fusion
  77.7 1.5 convolution_bitcast_fusion.1
  79.5 50.4 %all-reduce.7.cloned.1.call-done = (f32[1,512,512]{2,1,0:T(8,128)}, f32[1,512,512]{2,1,0:T(8,128)}) async-done(((f32[1,512,512]{2,1,0:T(8,128)}, f32[1,512,512]{2,1,0:T(8,128)}), (f32[1,512,512]{2,1,0:T(8,128)}, f32[1,512,512]{2,1,0:T(8,128)})) %all-reduce.7.cloned.1.call-update) | async-done | bytes 2097168 | tf_op jit(solution)/shard_map/psum | solution.py:71
  131.1 104.9 %all-reduce.5.cloned.1.call-done = (f32[1,512,512]{2,1,0:T(8,128)}, f32[1,512,512]{2,1,0:T(8,128)}) async-done(((f32[1,512,512]{2,1,0:T(8,128)}, f32[1,512,512]{2,1,0:T(8,128)}), (f32[1,512,512]{2,1,0:T(8,128)}, f32[1,512,512]{2,1,0:T(8,128)})) %all-reduce.5.cloned.1.call-update) | async-done | bytes 2097168 | tf_op jit(solution)/shard_map/psum | solution.py:71
  236.0 7.6 %fusion.2 = (f32[2,8,4096]{2,1,0:T(8,128)S(1)}, bf16[512,4096]{1,0:T(8,128)(2,1)}) fusion(f32[2,32,4096]{2,1,0:T(8,128)} %convert_element_type.132, bf16[512,4096]{1,0:T(8,128)(2,1)} %param.15, bf16[512,512]{1,0:T(8,128)(2,1)S(1)} %convolution_convert_fusion.3, f32[1,512,512]{2,1,0:T(8,128)} %get-tuple-element.6, f32[512]{0:T(512)S(1)} %bitcast.114), kind=kOutput, calls=%fused_computation.12 | convolution fusion | flops 2425552896 | bytes 11274240 | tf_op jit(solution)/shard_map/dot_general | solution.py:78
  243.6 7.4 %fusion = (f32[2,8,4096]{2,1,0:T(8,128)S(1)}, bf16[512,4096]{1,0:T(8,128)(2,1)}) fusion(f32[2,32,4096]{2,1,0:T(8,128)S(1)} %convert_element_type.123, bf16[512,4096]{1,0:T(8,128)(2,1)} %param.15, bf16[512,512]{1,0:T(8,128)(2,1)S(1)} %convolution_convert_fusion.5, f32[1,512,512]{2,1,0:T(8,128)} %get-tuple-element.5, f32[512]{0:T(512)S(1)} %bitcast.113), kind=kOutput, calls=%fused_computation.10 | convolution fusion | flops 2425552896 | bytes 11274240 | tf_op jit(solution)/shard_map/dot_general | solution.py:78
  250.9 4.6 %fusion.1 = (bf16[2,32,4096]{2,1,0:T(8,128)(2,1)S(1)}, bf16[2,32,4096]{2,1,0:T(8,128)(2,1)S(1)}) fusion(bf16[2,8,32,4096]{3,2,1,0:T(8,128)(2,1)} %bitcast.106, f32[2,8,4096]{2,1,0:T(8,128)S(1)} %convert_element_type.136, bf16[2,8,32,4096]{3,2,1,0:T(8,128)(2,1)} %bitcast.105), kind=kLoop, calls=%fused_computation.11 | loop fusion | flops 12058624 | bytes 9699328 | tf_op jit(solution)/shard_map/reduce_sum | solution.py:87
  257.6 29.4 %all_to_all.63 = bf16[2,2,8,16384]{3,1,0,2:T(2,128)(2,1)S(1)} all-to-all(bf16[2,2,8,16384]{3,1,0,2:T(2,128)(2,1)S(1)} %copy.57), channel_id=1, replica_groups=mesh['ka'=8,'band'=4] {'ka'}, dimensions={2} | all-to-all | bytes 2097152 | tf_op jit(solution)/shard_map/all_to_all | solution.py:94
  293.0 3.6 %all-to-all-start.3 = ((bf16[8,2,16384]{2,1,0:T(2,128)(2,1)}), bf16[8,2,16384]{2,1,0:T(2,128)(2,1)S(1)}, u32[]{:S(2)}, u32[]{:S(2)}) async-start(bf16[8,2,16384]{2,1,0:T(2,128)(2,1)} %reshape.317), calls=%async_computation.4 | async-start | bytes 1048576 | tf_op jit(solution)/shard_map/all_to_all | solution.py:98
  297.6 23.3 %reduce-scatter.2.cloned.1.call-done = bf16[2,8,1024]{2,1,0:T(8,128)(2,1)} async-done(((bf16[2,8,4096]{2,1,0:T(8,128)(2,1)}), bf16[2,8,1024]{2,1,0:T(8,128)(2,1)}) %reduce-scatter.2.cloned.1.call-update) | async-done | bytes 32784 | tf_op jit(solution)/shard_map/reduce_scatter | solution.py:102
  320.9 1.4 multiply_convert_fusion.6
  322.8 3.3 reduce
  326.7 1.2 reshape.232
  (71 shorter events, 19.4 us)
Async XLA Ops:
  7.2 33.8 %copy-start = (f32[16,32]{1,0:T(8,128)S(1)}, f32[16,32]{1,0:T(8,128)}, u32[]{:S(2)}) copy-start(f32[16,32]{1,0:T(8,128)} %param.12) | copy-start | bytes 6148
  10.0 21.8 %all-to-all-start = ((bf16[2,8,16384]{2,0,1:T(2,128)(2,1)}), bf16[2,8,16384]{2,0,1:T(2,128)(2,1)S(1)}, u32[]{:S(2)}, u32[]{:S(2)}) async-start(bf16[2,8,16384]{2,0,1:T(2,128)(2,1)} %copy.50), calls=%async_computation | async-start | bytes 1048576 | tf_op jit(solution)/shard_map/all_to_all | solution.py:49
  33.7 6.2 %copy-start.3 = (s32[2,16]{1,0:T(2,128)S(1)}, s32[2,16]{1,0:T(2,128)}, u32[]{:S(2)}) copy-start(s32[2,16]{1,0:T(2,128)} %param.13) | copy-start | bytes 388
  33.7 7.9 %copy-start.5 = (f32[2,8]{1,0:T(2,128)S(1)}, f32[2,8]{1,0:T(2,128)}, u32[]{:S(2)}) copy-start(f32[2,8]{1,0:T(2,128)} %param.11) | copy-start | bytes 196
  36.1 29.6 %all-to-all-start.1 = ((bf16[2,16,1,16384]{3,0,2,1:T(2,128)(2,1)}), bf16[2,16,1,16384]{3,0,2,1:T(2,128)(2,1)S(1)}, u32[]{:S(2)}, u32[]{:S(2)}) async-start(bf16[2,16,1,16384]{3,0,2,1:T(2,128)(2,1)} %copy.51), calls=%async_computation.1 | async-start | bytes 2097152 | tf_op jit(solution)/shard_map/all_to_all | solution.py:46
  39.7 90.2 %all-reduce.7.cloned.1.call-start = ((), (), s32[]{:S(2)}) async-start(), calls=%async_computation.7 | async-start | bytes 4194304 | tf_op jit(solution)/shard_map/psum | solution.py:71
  65.6 3.5 %copy-start.2 = (bf16[2,8,4096]{2,1,0:T(8,128)(2,1)S(1)}, bf16[2,8,4096]{2,1,0:T(8,128)(2,1)}, u32[]{:S(2)}) copy-start(bf16[2,8,4096]{2,1,0:T(8,128)(2,1)} %param.9) | copy-start | bytes 393220
  69.2 2.2 copy-start.1
  76.1 53.8 %copy-start.4 = (f32[2,512]{1,0:T(2,128)S(1)}, f32[2,512]{1,0:T(2,128)}, u32[]{:S(2)}) copy-start(f32[2,512]{1,0:T(2,128)} %param.14) | copy-start | bytes 12292
  79.3 156.7 %all-reduce.5.cloned.1.call-start = ((), (), s32[]{:S(2)}) async-start(), calls=%async_computation.6 | async-start | bytes 4194304 | tf_op jit(solution)/shard_map/psum | solution.py:71
  293.0 29.3 %all-to-all-start.3 = ((bf16[8,2,16384]{2,1,0:T(2,128)(2,1)}), bf16[8,2,16384]{2,1,0:T(2,128)(2,1)S(1)}, u32[]{:S(2)}, u32[]{:S(2)}) async-start(bf16[8,2,16384]{2,1,0:T(2,128)(2,1)} %reshape.317), calls=%async_computation.4 | async-start | bytes 1048576 | tf_op jit(solution)/shard_map/all_to_all | solution.py:98
  296.5 24.3 %reduce-scatter.2.cloned.1.call-start = ((), (), s32[]{:S(2)}) async-start(), calls=%async_computation.5 | async-start | bytes 163840 | tf_op jit(solution)/shard_map/reduce_scatter | solution.py:102
Sparse Core Ops, SparseCore 0:
  79.4 50.4 all-reduce.6
  133.5 102.3 all-reduce.4
  299.8 21.0 reduce-scatter.1
